TPU v7x, 512 devices: a whole 4x8x8 slice. The times are simulated.
512 devices in a mesh: gx: 64 (over z_lo, y, core), gy: 8 (over x, z_hi).
Axes of the slice: x: 4, y: 8, z: 8 (z_hi: 2, z_lo: 4; z = z_hi * 4 + z_lo), core: 2. Of those that a mesh axis runs over, the one named last changes fastest.
Arguments:
- forward_field: bfloat16 [2560, 128, 128], P('gy', 'gx'), may hold values from -6 to 6
- adjoint_field: bfloat16 [2560, 128, 128], P('gy', 'gx'), may hold values from -6 to 6
- row_scale: float32 [2560, 128], P('gy', 'gx'), may hold values from 0.5 to 2
- station_block: bfloat16 [2560, 2560], P('gy'), may hold values from -0.15625 to 0.15625
- jacobian_block: bfloat16 [2560, 2560], P('gy'), may hold values from -0.15625 to 0.15625
- shock_stations: int32 [16], replicated, may hold values from 0 to 127, as said below
Outputs:
- forward_image: bfloat16 [2560, 128, 128], P('gy', 'gx')
- adjoint_image: bfloat16 [2560, 128, 128], P('gy', 'gx')
Inputs may be any that keep to these rules, and one draw needn't show every extreme that they name: `shock_stations`: station indices, repeats possible; station 0 and station 128 - 1 are always listed.
All inputs are finite; a program needn't handle non-finite values.
Results may differ from a plain program's by a relative error of at most 0.013.
Values may be sent and summed in bfloat16 or wider, within the bound.
A program may use at most 64 MiB of HBM per device.

v0:
```python
import jax
import jax.numpy as jnp
from jax import lax
from jax.sharding import PartitionSpec as P

far_coeff = 1.0 / 12.0
near_coeff = 8.0 / 12.0
shock_gain = 0.5


def with_halo(block, sides, width):
    for axis, dim in sides:
        count = lax.axis_size(axis)
        forward = [(i, i + 1) for i in range(count - 1)]
        backward = [(target, source) for source, target in forward]
        low = lax.ppermute(
            lax.slice_in_dim(block, block.shape[dim] - width, None, axis=dim), axis, forward
        )
        high = lax.ppermute(lax.slice_in_dim(block, 0, width, axis=dim), axis, backward)
        block = jnp.concatenate([low, block, high], axis=dim)
    return block


def streamwise(ext, count):
    values = ext.astype(jnp.float32)
    return (
        far_coeff * values[:, 0:count]
        - near_coeff * values[:, 1 : 1 + count]
        + near_coeff * values[:, 3 : 3 + count]
        - far_coeff * values[:, 4 : 4 + count]
    )


def transposed(ext, count):
    values = ext.astype(jnp.float32)
    return (
        far_coeff * values[:, 4 : 4 + count]
        - near_coeff * values[:, 3 : 3 + count]
        + near_coeff * values[:, 1 : 1 + count]
        - far_coeff * values[:, 0:count]
    )


def second_diff(ext, count):
    values = ext.astype(jnp.float32)
    return values[:, 1 : 1 + count] - 2.0 * values[:, 2 : 2 + count] + values[:, 3 : 3 + count]


def left_dot(matrix, other):
    return lax.dot_general(
        matrix, other, (((0,), (0,)), ((), ())), preferred_element_type=jnp.float32
    )


def local(forward_field, adjoint_field, row_scale, station_block, jacobian_block, shock_stations):
    own_rows = forward_field.shape[0]
    count = forward_field.shape[1]
    width = forward_field.shape[2]
    flat = count * width
    total_rows = station_block.shape[1]
    first = lax.axis_index("gx") * count
    station_ids = first - 2 + jnp.arange(count + 4, dtype=jnp.int32)
    sigma_ext = jnp.any(station_ids[:, None] == shock_stations[None, :], axis=1).astype(jnp.float32)
    sigma_own = sigma_ext[2 : 2 + count]
    pencils = lax.all_gather(forward_field, "gy", axis=0, tiled=True)
    pencil_ext = with_halo(pencils, (("gx", 1),), 2)
    slope = streamwise(pencil_ext, count).astype(jnp.bfloat16)
    centre = pencil_ext[:, 2 : 2 + count].reshape(total_rows, flat)
    dense = jnp.dot(station_block, centre, preferred_element_type=jnp.float32)
    flux = jnp.dot(
        jacobian_block, slope.reshape(total_rows, flat), preferred_element_type=jnp.float32
    )
    own_ext = lax.dynamic_slice_in_dim(pencil_ext, lax.axis_index("gy") * own_rows, own_rows, 0)
    w_ext = with_halo(adjoint_field, (("gx", 1),), 2)
    forward_out = row_scale[:, :, None] * dense.reshape(own_rows, count, width) + flux.reshape(
        own_rows, count, width
    )
    forward_out = forward_out + shock_gain * sigma_own[None, :, None] * second_diff(own_ext, count)
    back = transposed(w_ext, count).astype(jnp.bfloat16).reshape(own_rows, flat)
    scaled = (
        (row_scale[:, :, None] * adjoint_field.astype(jnp.float32))
        .astype(jnp.bfloat16)
        .reshape(own_rows, flat)
    )
    summed = lax.psum_scatter(
        (left_dot(station_block, scaled) + left_dot(jacobian_block, back)).astype(jnp.bfloat16),
        "gy",
        scatter_dimension=0,
        tiled=True,
    ).astype(jnp.float32)
    weighted = sigma_ext[None, :, None] * w_ext.astype(jnp.float32)
    adjoint_out = summed.reshape(own_rows, count, width) + shock_gain * second_diff(weighted, count)
    return (forward_out.astype(jnp.bfloat16), adjoint_out.astype(jnp.bfloat16))


def solution(mesh):
    in_specs = (
        P("gy", "gx", None),
        P("gy", "gx", None),
        P("gy", "gx"),
        P("gy", None),
        P("gy", None),
        P(),
    )
    out_specs = (P("gy", "gx", None), P("gy", "gx", None))
    return jax.shard_map(local, mesh=mesh, in_specs=in_specs, out_specs=out_specs, check_vma=False)
```

profile of v0, /device:TPU:6, one launch (start us, length us, event | category | flops | bytes accessed | tf_op | source)
XLA Modules:
  0.0 205.4 jit_solution(1199272171501167596)
XLA Ops:
  7.2 1.7 copy.57
  9.0 0.0 reduce-scatter.4.cloned.1.call-start
  9.0 0.9 copy.61
  10.0 1.7 collective-permute-start.2
  11.7 1.3 collective-permute-start.3
  13.0 2.5 %fusion.41 = f32[256,2560]{1,0:T(8,128)S(1)} fusion(bf16[320,2560]{1,0:T(8,128)(2,1)} %param.9, f32[320,2]{0,1:T(2,128)} %param.8, bf16[320,2,128]{2,1,0:T(2,128)(2,1)} %param.7), kind=kOutput, calls=%fused_computation.45 | convolution fusion | flops 419676160 | bytes 4426240 | tf_op jit(solution)/shard_map/dot_general | solution.py:50
  15.5 0.8 collective-permute-done.3
  16.4 0.1 maximum_convert_fusion
  16.4 0.9 fusion.1
  17.4 1.5 copy.71
  18.9 68.7 %all-gather.2.cloned.1.call-done = bf16[2560,2,128]{2,0,1:T(8,128)(2,1)} async-done(((bf16[320,2,128]{2,0,1:T(8,128)(2,1)}), bf16[2560,2,128]{2,0,1:T(8,128)(2,1)}) %all-gather.2.cloned.1.call-update) | async-done | bytes 1310736 | tf_op jit(solution)/shard_map/all_gather | solution.py:65
  87.5 2.5 %collective-permute-start = (bf16[2560,2,128]{2,0,1:T(8,128)(2,1)}, bf16[2560,2,128]{2,0,1:T(8,128)(2,1)}, u32[]{:S(2)}, u32[]{:S(2)}) collective-permute-start(bf16[2560,2,128]{2,0,1:T(8,128)(2,1)} %all-gather.2.cloned.1.call-done), channel_id=1, source_target_pairs={{0,8},{8,16},{16,24},{24,32},{32,40},{40,48},{48,56},{56,64},{64,7... | collective-permute-start | bytes 3932168 | tf_op jit(solution)/shard_map/ppermute | solution.py:16
  90.0 0.2 compare_reduce_fusion
  90.2 1.3 collective-permute-start.1
  91.5 0.1 slice_multiply_fusion.10
  91.6 1.1 broadcast_multiply_fusion
  92.7 1.4 copy.58
  94.1 89.7 %reduce-scatter.4.cloned.1.call-done = bf16[320,256]{1,0:T(8,128)(2,1)} async-done(((bf16[2560,256]{1,0:T(8,128)(2,1)}), bf16[320,256]{1,0:T(8,128)(2,1)}) %reduce-scatter.4.cloned.1.call-update) | async-done | bytes 163856 | tf_op jit(solution)/shard_map/reduce_scatter | solution.py:85
  183.8 1.3 fusion.29
  185.1 0.8 copy.70
  186.0 1.4 constant_dynamic-update-slice_fusion.2
  187.4 0.2 constant_dynamic-update-slice_fusion.1
  187.6 1.5 constant_dynamic-update-slice_fusion
  189.1 0.5 convert_element_type.42
  189.6 1.0 dynamic-slice_convert_fusion
  190.6 1.8 fusion.3
  192.5 1.6 copy.59
  194.1 0.6 convolution_bitcast_fusion
  194.7 0.8 copy-done.2
  195.5 0.4 copy-done.3
  195.9 1.8 fusion.24
  197.7 0.8 copy.69
  (18 shorter events, 0.1 us)
Async XLA Ops:
  7.2 9.3 %copy-start = (bf16[320,2560]{1,0:T(8,128)(2,1)S(1)}, bf16[320,2560]{1,0:T(8,128)(2,1)}, u32[]{:S(2)}) copy-start(bf16[320,2560]{1,0:T(8,128)(2,1)} %param.10) | copy-start | bytes 4915204
  7.2 80.3 %all-gather.2.cloned.1.call-start = ((), (), s32[]{:S(2)}) async-start(), calls=%async_computation.1 | async-start | bytes 1474560 | tf_op jit(solution)/shard_map/all_gather | solution.py:65
  9.0 174.9 %reduce-scatter.4.cloned.1.call-start = ((), (), s32[]{:S(2)}) async-start(), calls=%async_computation.2 | async-start | bytes 1474560 | tf_op jit(solution)/shard_map/reduce_scatter | solution.py:85
  10.0 5.6 %collective-permute-start.2 = (bf16[320,2,128]{2,0,1:T(8,128)(2,1)S(1)}, bf16[320,2,128]{2,0,1:T(8,128)(2,1)S(1)}, u32[]{:S(2)}, u32[]{:S(2)}) collective-permute-start(bf16[320,2,128]{2,0,1:T(8,128)(2,1)S(1)} %copy.61), channel_id=1, source_target_pairs={{0,8},{8,16},{16,24},{24,32},{32,40},{40,48},{48,56},{56,64},{64,7... | collective-permute-start | bytes 491528 | tf_op jit(solution)/shard_map/ppermute | solution.py:16
  11.7 4.6 %collective-permute-start.3 = (bf16[320,2,128]{2,0,1:T(8,128)(2,1)S(1)}, bf16[320,2,128]{2,0,1:T(8,128)(2,1)S(1)}, u32[]{:S(2)}, u32[]{:S(2)}) collective-permute-start(bf16[320,2,128]{2,0,1:T(8,128)(2,1)S(1)} %copy.61), channel_id=1, source_target_pairs={{8,0},{16,8},{24,16},{32,24},{40,32},{48,40},{56,48},{64,56},{72,6... | collective-permute-start | bytes 491528 | tf_op jit(solution)/shard_map/ppermute | solution.py:19
  17.4 72.6 %copy-start.5 = (s32[16]{0:T(128)S(1)}, s32[16]{0:T(128)}, u32[]{:S(2)}) copy-start(s32[16]{0:T(128)} %param.11) | copy-start | bytes 196
  87.5 5.1 %copy-start.1 = (bf16[2560,2,128]{2,0,1:T(8,128)(2,1)S(1)}, bf16[2560,2,128]{2,0,1:T(8,128)(2,1)}, u32[]{:S(2)}) copy-start(bf16[2560,2,128]{2,0,1:T(8,128)(2,1)} %all-gather.2.cloned.1.call-done) | copy-start | bytes 3932164
  87.5 98.5 %collective-permute-start = (bf16[2560,2,128]{2,0,1:T(8,128)(2,1)}, bf16[2560,2,128]{2,0,1:T(8,128)(2,1)}, u32[]{:S(2)}, u32[]{:S(2)}) collective-permute-start(bf16[2560,2,128]{2,0,1:T(8,128)(2,1)} %all-gather.2.cloned.1.call-done), channel_id=1, source_target_pairs={{0,8},{8,16},{16,24},{24,32},{32,40},{40,48},{48,56},{56,64},{64,7... | collective-permute-start | bytes 3932168 | tf_op jit(solution)/shard_map/ppermute | solution.py:16
  90.2 97.4 %collective-permute-start.1 = (bf16[2560,2,128]{2,0,1:T(8,128)(2,1)}, bf16[2560,2,128]{2,0,1:T(8,128)(2,1)}, u32[]{:S(2)}, u32[]{:S(2)}) collective-permute-start(bf16[2560,2,128]{2,0,1:T(8,128)(2,1)} %all-gather.2.cloned.1.call-done), channel_id=1, source_target_pairs={{8,0},{16,8},{24,16},{32,24},{40,32},{48,40},{56,48},{64,56},{72,6... | collective-permute-start | bytes 3932168 | tf_op jit(solution)/shard_map/ppermute | solution.py:19
  194.1 1.4 copy-start.2
  194.1 1.8 copy-start.3
  194.1 1.8 copy-start.4
Sparse Core Ops, SparseCore 0:
  11.8 75.6 all-gather.1
  92.1 91.6 reduce-scatter.3
where the time goes:
time: 206 us; the launch traced here: 205 us
  waiting for transfers between devices  159 us (77%)
  between operations  14.2 us (7%)
  local copies, waits for them, and re-layouts  13.1 us (6%)
  starting transfers between devices  6.87 us (3%)
  other arithmetic  6.16 us (3%)
  matrix products  5.84 us (3%)
    reduce_scatter x1, waiting for transfers between devices, local(): lax.psum_scatter((left_dot(station_block, scaled) + left_dot(jacobian_blo...  89.7 us
    all_gather x1, waiting for transfers between devices, local(): pencils = lax.all_gather(forward_field, 'gy', axis=0, tiled=True)  68.7 us
    unnamed x19, local copies, waits for them, and re-layouts  8.54 us
    ppermute x2, starting transfers between devices, with_halo(): lax.ppermute(lax.slice_in_dim(block, block.shape[dim] - width, None, axis...  4.21 us
  transfers between devices with their start and end apart: 6, of which 3 were waited for; matrix products, arithmetic and copies ran while one was open for 6% of the time, Pallas kernels for 0%

commit v1 on v0

v1 whole, which is shorter than its diff:
```python
import functools

import jax
import jax.numpy as jnp
from jax import lax
from jax.experimental import pallas as pl
from jax.experimental.pallas import tpu as pltpu
from jax.sharding import PartitionSpec as P

FAR = 1.0 / 12.0
NEAR = 8.0 / 12.0
SHOCK_GAIN = 0.5
N_X = 4
N_Z = 8
N_ZLO = 4
MESH = pl.DeviceIdType.MESH
N_MSG = 40


def kernel(
    n_gx,
    q_ref, w_ref, scale_ref, shock_ref, a_hbm, j_hbm,
    fo_ref, ao_ref,
    aj, qb, tb, sb, facc, wl, wr, zq, rx, acc, zs, zt, rz, pr, pn,
    local_sem, send_sem, recv_sem,
):
    f32, bf16 = jnp.float32, jnp.bfloat16
    rows, flat = q_ref.shape
    half = rows // 2
    width = flat // 2
    inner = n_gx // N_ZLO
    up, lo = pl.ds(0, half), pl.ds(half, half)
    c0, c1 = slice(0, width), slice(width, flat)

    gx, gy = lax.axis_index("gx"), lax.axis_index("gy")
    x, h = gy // 2, gy % 2
    z = h * N_ZLO + gx // inner
    xs = [(x + d) % N_X for d in range(N_X)]

    def at_z(zz):
        return {"gx": (zz % N_ZLO) * inner + gx % inner, "gy": x * 2 + zz // N_ZLO}

    right = {"gx": gx, "gy": xs[1] * 2 + h}
    left = {"gx": gx, "gy": xs[3] * 2 + h}
    z_up, z_dn = at_z((z + 2) % N_Z), at_z((z + N_Z - 2) % N_Z)
    g_next = {"gx": (gx + 1) % n_gx, "gy": gy}
    g_prev = {"gx": (gx + n_gx - 1) % n_gx, "gy": gy}

    started = []

    def message(i, src, dst, dev):
        return pltpu.make_async_remote_copy(
            src_ref=src, dst_ref=dst, send_sem=send_sem.at[i], recv_sem=recv_sem.at[i],
            device_id=dev, device_id_type=MESH,
        )

    def send(i, src, dst, dev):
        copy = message(i, src, dst, dev)
        copy.start()
        started.append(copy)

    def arrived(i, dst, dev):
        message(i, dst, dst, dev).wait_recv()

    load_a = pltpu.make_async_copy(a_hbm, aj.at[pl.ds(0, rows)], local_sem.at[0])
    load_j = pltpu.make_async_copy(j_hbm, aj.at[pl.ds(rows, rows)], local_sem.at[1])
    load_a.start()
    load_j.start()

    barrier = pltpu.get_barrier_semaphore()
    for dev in (right, left, z_up, z_dn, g_next, g_prev):
        pl.semaphore_signal(barrier, inc=1, device_id=dev, device_id_type=MESH)
    pl.semaphore_wait(barrier, 6)

    send(2, q_ref.at[up], zq.at[0], z_up)
    send(3, q_ref.at[lo], zq.at[1], z_dn)
    send(4, q_ref.at[up], qb.at[gy, up], right)
    send(6, q_ref.at[lo], qb.at[gy, lo], left)
    send(0, w_ref, wl, g_next)
    send(1, w_ref, wr, g_prev)
    send(5, q_ref.at[lo], qb.at[gy, lo], right)
    send(7, q_ref.at[up], qb.at[gy, up], left)
    qb[gy] = q_ref[...]

    has_prev = jnp.where(gx > 0, 1.0, 0.0).astype(f32)
    has_next = jnp.where(gx < n_gx - 1, 1.0, 0.0).astype(f32)
    arrived(0, wl, g_prev)
    arrived(1, wr, g_next)
    w0, w1 = w_ref[:, c0].astype(f32), w_ref[:, c1].astype(f32)
    l0, l1 = wl[:, c0].astype(f32) * has_prev, wl[:, c1].astype(f32) * has_prev
    r0, r1 = wr[:, c0].astype(f32) * has_next, wr[:, c1].astype(f32) * has_next
    s0, s1 = scale_ref[:, 0:1], scale_ref[:, 1:2]
    sb[pl.ds(0, rows), c0] = (s0 * w0).astype(bf16)
    sb[pl.ds(0, rows), c1] = (s1 * w1).astype(bf16)
    sb[pl.ds(rows, rows), c0] = (((FAR * r0 - NEAR * w1) + NEAR * l1) - FAR * l0).astype(bf16)
    sb[pl.ds(rows, rows), c1] = (((FAR * r1 - NEAR * r0) + NEAR * w0) - FAR * l1).astype(bf16)
    load_a.wait()
    load_j.wait()

    def columns(d):
        return pl.ds(pl.multiple_of(xs[d] * (2 * rows), 128), 2 * rows)

    def transposed_block(d):
        t = lax.dot_general(
            aj[:, columns(d)], sb[...], (((0,), (0,)), ((), ())), preferred_element_type=f32
        ).astype(bf16)
        tb[2 * d] = t[:rows]
        tb[2 * d + 1] = t[rows:]

    transposed_block(2)
    gl, gr = xs[3] * 2 + h, xs[1] * 2 + h
    arrived(4, qb.at[gl, up], left)
    send(8, qb.at[gl, up], qb.at[gl, up], right)
    arrived(6, qb.at[gr, lo], right)
    send(9, qb.at[gr, lo], qb.at[gr, lo], left)

    def first_far(k, base):
        part = 4 + (1 - h if k == 0 else h)
        send(base, tb.at[part, up], rx.at[k, 0, 0], right)
        send(base + 1, tb.at[part, lo], rx.at[k, 1, 0], left)

    def first_near(k, base):
        hh = 1 - h if k == 0 else h
        send(base + 2, tb.at[2 + hh, lo], rx.at[k, 0, 1], right)
        send(base + 3, tb.at[6 + hh, up], rx.at[k, 1, 1], left)

    def second(k, base):
        hh = 1 - h if k == 0 else h
        arrived(base, rx.at[k, 0, 0], left)
        acc[k, 0] = (tb[2 + hh, up, :].astype(f32) + rx[k, 0, 0].astype(f32)).astype(bf16)
        arrived(base + 1, rx.at[k, 1, 0], right)
        acc[k, 1] = (tb[6 + hh, lo, :].astype(f32) + rx[k, 1, 0].astype(f32)).astype(bf16)
        send(base + 4, acc.at[k, 0], rx.at[k, 0, 2], right)
        send(base + 5, acc.at[k, 1], rx.at[k, 1, 2], left)

    def summed(k, base):
        hh = 1 - h if k == 0 else h
        arrived(base + 2, rx.at[k, 0, 1], left)
        arrived(base + 3, rx.at[k, 1, 1], right)
        arrived(base + 4, rx.at[k, 0, 2], left)
        arrived(base + 5, rx.at[k, 1, 2], right)
        top = (tb[hh, up, :].astype(f32) + rx[k, 0, 2].astype(f32)) + rx[k, 1, 1].astype(f32)
        bottom = (tb[hh, lo, :].astype(f32) + rx[k, 0, 1].astype(f32)) + rx[k, 1, 2].astype(f32)
        return top, bottom

    transposed_block(1)
    first_far(0, 10)
    gp = x * 2 + (1 - h)
    origin_dn = x * 2 + ((z + N_Z - 2) % N_Z) // N_ZLO
    origin_up = x * 2 + ((z + 2) % N_Z) // N_ZLO
    arrived(2, zq.at[0], z_dn)
    send(22, zq.at[0], qb.at[origin_dn, up], z_up)
    arrived(3, zq.at[1], z_up)
    send(23, zq.at[1], qb.at[origin_up, lo], z_dn)
    transposed_block(3)
    first_near(0, 10)
    transposed_block(0)
    second(0, 10)

    arrived(22, qb.at[gp, up], z_dn)
    send(24, qb.at[gp, up], qb.at[gp, up], right)
    send(27, qb.at[gp, up], qb.at[gp, up], left)
    arrived(23, qb.at[gp, lo], z_up)
    send(26, qb.at[gp, lo], qb.at[gp, lo], left)
    send(25, qb.at[gp, lo], qb.at[gp, lo], right)

    top, bottom = summed(0, 10)
    zs[up, :] = top.astype(bf16)
    zs[lo, :] = bottom.astype(bf16)

    def forward_block(d):
        part = jnp.dot(
            aj[:, columns(d)],
            qb[pl.ds(xs[d] * 2, 2)].reshape(2 * rows, flat),
            preferred_element_type=f32,
        )
        facc[...] = part if d == 0 else facc[...] + part

    forward_block(0)
    send(30, zs.at[up], zt.at[0], z_up)
    send(31, zs.at[lo], zt.at[1], z_dn)
    first_far(1, 16)
    first_near(1, 16)

    gl2, gr2 = xs[3] * 2 + (1 - h), xs[1] * 2 + (1 - h)
    arrived(24, qb.at[gl2, up], left)
    send(28, qb.at[gl2, up], qb.at[gl2, up], right)
    arrived(26, qb.at[gr2, lo], right)
    send(29, qb.at[gr2, lo], qb.at[gr2, lo], left)
    second(1, 16)

    arrived(30, zt.at[0], z_dn)
    send(32, zt.at[0], rz.at[up], z_up)
    arrived(31, zt.at[1], z_up)
    send(33, zt.at[1], rz.at[lo], z_dn)

    arrived(5, qb.at[gl, lo], left)
    arrived(25, qb.at[gl2, lo], left)
    forward_block(3)
    arrived(7, qb.at[gr, up], right)
    arrived(27, qb.at[gr2, up], right)
    forward_block(1)
    far_own, far_other = xs[2] * 2 + h, xs[2] * 2 + (1 - h)
    arrived(8, qb.at[far_own, up], left)
    arrived(9, qb.at[far_own, lo], right)
    arrived(28, qb.at[far_other, up], left)
    arrived(29, qb.at[far_other, lo], right)
    forward_block(2)

    def sigma(offset):
        station = gx * 2 + offset
        hit = jnp.where(shock_ref[0] == station, 1.0, 0.0)
        for k in range(1, shock_ref.shape[0]):
            hit = jnp.where(shock_ref[k] == station, 1.0, hit)
        return hit.astype(f32)

    sig = [sigma(o) for o in (-1, 0, 1, 2)]
    q0, q1 = q_ref[:, c0].astype(f32), q_ref[:, c1].astype(f32)
    flux = pl.ds(rows, rows)
    p0, p1 = facc[flux, c0], facc[flux, c1]
    pn[0, :, c0] = ((FAR * p0 - NEAR * p1) + (SHOCK_GAIN * sig[3]) * q1).astype(bf16)
    pn[0, :, c1] = (FAR * p1).astype(bf16)
    pn[1, :, c0] = (-FAR * p0).astype(bf16)
    pn[1, :, c1] = ((NEAR * p0 - FAR * p1) + (SHOCK_GAIN * sig[0]) * q0).astype(bf16)
    send(34, pn.at[0], pr.at[0], g_next)
    send(35, pn.at[1], pr.at[1], g_prev)

    top, bottom = summed(1, 16)
    add0 = SHOCK_GAIN * ((sig[0] * l1 - 2.0 * sig[1] * w0) + sig[2] * w1)
    add1 = SHOCK_GAIN * ((sig[1] * w0 - 2.0 * sig[2] * w1) + sig[3] * r0)
    arrived(32, rz.at[up], z_dn)
    top = top + rz[up, :].astype(f32)
    ao_ref[up, c0] = (top[:, c0] + add0[:half]).astype(bf16)
    ao_ref[up, c1] = (top[:, c1] + add1[:half]).astype(bf16)
    arrived(33, rz.at[lo], z_up)
    bottom = bottom + rz[lo, :].astype(f32)
    ao_ref[lo, c0] = (bottom[:, c0] + add0[half:]).astype(bf16)
    ao_ref[lo, c1] = (bottom[:, c1] + add1[half:]).astype(bf16)

    base0 = s0 * facc[pl.ds(0, rows), c0] + NEAR * p1 + (SHOCK_GAIN * sig[1]) * (q1 - 2.0 * q0)
    base1 = s1 * facc[pl.ds(0, rows), c1] - NEAR * p0 + (SHOCK_GAIN * sig[2]) * (q0 - 2.0 * q1)
    arrived(34, pr.at[0], g_prev)
    arrived(35, pr.at[1], g_next)
    fo_ref[:, c0] = (
        base0 + has_prev * pr[0, :, c0].astype(f32) + has_next * pr[1, :, c0].astype(f32)
    ).astype(bf16)
    fo_ref[:, c1] = (
        base1 + has_prev * pr[0, :, c1].astype(f32) + has_next * pr[1, :, c1].astype(f32)
    ).astype(bf16)

    for copy in started:
        copy.wait_send()


def local(n_gx, q, w, row_scale, station_block, jacobian_block, shock_stations):
    rows, count, width = q.shape
    flat = count * width
    total = station_block.shape[1]
    bf16 = jnp.bfloat16
    vmem = pl.BlockSpec(memory_space=pltpu.VMEM)
    hbm = pl.BlockSpec(memory_space=pl.ANY)
    half = rows // 2
    out = jax.ShapeDtypeStruct((rows, flat), bf16)
    fo, ao = pl.pallas_call(
        functools.partial(kernel, n_gx),
        out_shape=(out, out),
        in_specs=[vmem, vmem, vmem, pl.BlockSpec(memory_space=pltpu.SMEM), hbm, hbm],
        out_specs=(vmem, vmem),
        scratch_shapes=[
            pltpu.VMEM((2 * rows, total), bf16),
            pltpu.VMEM((2 * N_X, rows, flat), bf16),
            pltpu.VMEM((2 * N_X, rows, flat), bf16),
            pltpu.VMEM((2 * rows, flat), bf16),
            pltpu.VMEM((2 * rows, flat), jnp.float32),
            pltpu.VMEM((rows, flat), bf16),
            pltpu.VMEM((rows, flat), bf16),
            pltpu.VMEM((2, half, flat), bf16),
            pltpu.VMEM((2, 2, 3, half, flat), bf16),
            pltpu.VMEM((2, 2, half, flat), bf16),
            pltpu.VMEM((rows, flat), bf16),
            pltpu.VMEM((2, half, flat), bf16),
            pltpu.VMEM((rows, flat), bf16),
            pltpu.VMEM((2, rows, flat), bf16),
            pltpu.VMEM((2, rows, flat), bf16),
            pltpu.SemaphoreType.DMA((2,)),
            pltpu.SemaphoreType.DMA((N_MSG,)),
            pltpu.SemaphoreType.DMA((N_MSG,)),
        ],
        compiler_params=pltpu.CompilerParams(
            collective_id=0, has_side_effects=True, vmem_limit_bytes=40 * 1024 * 1024
        ),
    )(
        q.reshape(rows, flat), w.reshape(rows, flat), row_scale, shock_stations,
        station_block, jacobian_block,
    )
    return fo.reshape(rows, count, width), ao.reshape(rows, count, width)


def solution(mesh):
    in_specs = (
        P("gy", "gx", None),
        P("gy", "gx", None),
        P("gy", "gx"),
        P("gy", None),
        P("gy", None),
        P(),
    )
    out_specs = (P("gy", "gx", None), P("gy", "gx", None))
    return jax.shard_map(
        functools.partial(local, mesh.shape["gx"]),
        mesh=mesh, in_specs=in_specs, out_specs=out_specs, check_vma=False,
    )
```

time: 206 us -> 51 us (0.25)
  waiting for transfers between devices: 159 us -> 0 us
  Pallas kernels: 0 us -> 43.3 us
  between operations: 14.2 us -> 0.66 us
  starting transfers between devices: 6.87 us -> 0 us
  local copies, waits for them, and re-layouts: 13.1 us -> 6.78 us
  other arithmetic: 6.16 us -> 0 us
  matrix products: 5.84 us -> 0 us
    reduce_scatter x1 -> x0, waiting for transfers between devices: 89.7 us -> none  [local(): lax.psum_scatter((left_dot(station_block, scaled) + left_dot(jacobian_blo...]
    all_gather x1 -> x0, waiting for transfers between devices: 68.7 us -> none  [local(): pencils = lax.all_gather(forward_field, 'gy', axis=0, tiled=True)]
    pallas_call x0 -> x1, Pallas kernels: none -> 43.3 us  [local(): pl.pallas_call(functools.partial(kernel, n_gx), out_shape=(out, out), in_...]
    ppermute x4 -> x0, starting transfers between devices: 6.79 us -> none  [the longest x2 4.21 us: with_halo(): lax.ppermute(lax.slice_in_dim(block, block.shape[dim] - width, None, axis...]
    dot_general x4 -> x0, matrix products: 5.84 us -> none  [the longest x2 3.41 us: left_dot(): lax.dot_general(matrix, other, (((0,), (0,)), ((), ())), preferred_elemen...]
    convert_element_type x6 -> x0, other arithmetic: 4.8 us -> none  [the longest x1 1.84 us: local(): slope = streamwise(pencil_ext, count).astype(jnp.bfloat16)]
    unnamed x19 -> x7, local copies, waits for them, and re-layouts: 8.54 us -> 4.33 us
    reshape x0 -> x3, local copies, waits for them, and re-layouts: none -> 2.46 us  [the longest x2 1.42 us: local(): return (fo.reshape(rows, count, width), ao.reshape(rows, count, width))]
  transfers between devices with their start and end apart: 6 -> 0, of which waited for: 3 -> 0; matrix products, arithmetic and copies ran while one was open for 6% -> 0% of each run, Pallas kernels for 0% -> 0%
where the time goes in v1:
time: 51 us; the launch traced here: 50.8 us
  Pallas kernels  43.3 us (85%)
  local copies, waits for them, and re-layouts  6.78 us (13%)
  between operations  0.66 us (1%)
    pallas_call x1, Pallas kernels, local(): pl.pallas_call(functools.partial(kernel, n_gx), out_shape=(out, out), in_...  43.3 us
    unnamed x7, local copies, waits for them, and re-layouts  4.33 us
    reshape x2, local copies, waits for them, and re-layouts, local(): return (fo.reshape(rows, count, width), ao.reshape(rows, count, width))  1.42 us
    reshape x1, local copies, waits for them, and re-layouts, local(): w.reshape(rows, flat)  1.04 us

profile of v1, /device:TPU:6, one launch (start us, length us, event | category | flops | bytes accessed | tf_op | source)
XLA Modules:
  0.0 50.8 jit_solution(8188000914554093077)
XLA Ops:
  0.6 0.8 %copy.8.scale_ref = f32[320,2]{1,0:T(8,128)S(1)} copy(f32[320,2]{0,1:T(2,128)} %param.8) | data formatting | bytes 5120 | tf_op args[2]
  1.5 1.0 %copy_bitcast_fusion = (bf16[320,256]{1,0:T(8,128)(2,1)S(1)}, bf16[320,256]{1,0:T(8,128)(2,1)S(1)}) fusion(bf16[40,8,2,128]{3,2,1,0:T(2,128)(2,1)} %bitcast.6, bf16[40,8,2,128]{3,2,1,0:T(2,128)(2,1)} %bitcast.7), kind=kLoop, calls=%fused_computation | loop fusion | bytes 655360 | tf_op jit(solution)/shard_map/reshape | solution.py:293
  2.5 0.0 copy-start
  2.5 1.4 %copy-done = bf16[320,2560]{1,0:T(8,128)(2,1)S(1)} copy-done((bf16[320,2560]{1,0:T(8,128)(2,1)S(1)}, bf16[320,2560]{1,0:T(8,128)(2,1)}, u32[]{:S(2)}) %copy-start) | copy-done | bytes 1638424
  3.9 0.0 copy-start.1
  3.9 1.4 %copy-done.1 = bf16[320,2560]{1,0:T(8,128)(2,1)S(1)} copy-done((bf16[320,2560]{1,0:T(8,128)(2,1)S(1)}, bf16[320,2560]{1,0:T(8,128)(2,1)}, u32[]{:S(2)}) %copy-start.1) | copy-done | bytes 1638424
  5.4 0.0 copy-start.2
  5.4 0.7 %copy-done.2 = s32[16]{0:T(128)S(1)} copy-done((s32[16]{0:T(128)S(1)}, s32[16]{0:T(128)}, u32[]{:S(2)}) %copy-start.2) | copy-done | bytes 88
  6.0 43.3 %shard_map.77 = (bf16[320,256]{1,0:T(8,128)(2,1)S(1)}, bf16[320,256]{1,0:T(8,128)(2,1)S(1)}) custom-call(bf16[320,256]{1,0:T(8,128)(2,1)S(1)} %get-tuple-element.7.q_ref, bf16[320,256]{1,0:T(8,128)(2,1)S(1)} %get-tuple-element.6.w_ref, f32[320,2]{1,0:T(8,128)S(1)} %copy.8.scale_ref, s32[16]{0:T(128)S(1)} %copy-done.2, bf16[320,2560]{1,0:T(8,128)(2,1)S(1)} %copy-done, ...), custom_call_target="tpu_custom_call" | custom-call | tf_op jit(solution)/shard_map/pallas_call | solution.py:264
  49.3 0.7 %reshape.18 = bf16[320,2,128]{2,1,0:T(2,128)(2,1)} reshape(bf16[320,256]{1,0:T(8,128)(2,1)S(1)} %get-tuple-element.4) | data formatting | bytes 327680 | tf_op jit(solution)/shard_map/reshape | solution.py:296
  50.1 0.7 %reshape.19 = bf16[320,2,128]{2,1,0:T(2,128)(2,1)} reshape(bf16[320,256]{1,0:T(8,128)(2,1)S(1)} %get-tuple-element.5) | data formatting | bytes 327680 | tf_op jit(solution)/shard_map/reshape | solution.py:296
Async XLA Ops:
  2.5 1.4 %copy-start = (bf16[320,2560]{1,0:T(8,128)(2,1)S(1)}, bf16[320,2560]{1,0:T(8,128)(2,1)}, u32[]{:S(2)}) copy-start(bf16[320,2560]{1,0:T(8,128)(2,1)} %a_hbm.1) | copy-start | bytes 4915204
  3.9 1.4 %copy-start.1 = (bf16[320,2560]{1,0:T(8,128)(2,1)S(1)}, bf16[320,2560]{1,0:T(8,128)(2,1)}, u32[]{:S(2)}) copy-start(bf16[320,2560]{1,0:T(8,128)(2,1)} %j_hbm.1) | copy-start | bytes 4915204
  5.4 0.7 %copy-start.2 = (s32[16]{0:T(128)S(1)}, s32[16]{0:T(128)}, u32[]{:S(2)}) copy-start(s32[16]{0:T(128)} %shock_ref.1) | copy-start | bytes 196

commit v2 on v1

v2 whole, which is shorter than its diff:
```python
import functools

import jax
import jax.numpy as jnp
from jax import lax
from jax.experimental import pallas as pl
from jax.experimental.pallas import tpu as pltpu
from jax.sharding import PartitionSpec as P

FAR = 1.0 / 12.0
NEAR = 8.0 / 12.0
SHOCK_GAIN = 0.5
N_X = 4
N_Z = 8
N_ZLO = 4
MESH = pl.DeviceIdType.MESH
N_MSG = 64
N_PIECE = 4


def kernel(
    n_gx,
    q_ref, w_ref, scale_hbm, shock_hbm, a_hbm, j_hbm,
    fo_ref, ao_ref,
    scale_ref, shock_ref, aj, qb, tb, sb, facc, wl, wr, rx, acc, zs, rz, pr, pn,
    local_sem, send_sem, recv_sem,
):
    f32, bf16 = jnp.float32, jnp.bfloat16
    rows, flat = q_ref.shape
    tall = rows // N_PIECE
    width = flat // 2
    span = [pl.ds(p * tall, tall) for p in range(N_PIECE)]
    n_up = N_PIECE // 2
    c0, c1 = slice(0, width), slice(width, flat)

    gx, gy = lax.axis_index("gx"), lax.axis_index("gy")
    x, h = gy // 2, gy % 2
    xs = [(x + d) % N_X for d in range(N_X)]

    right = {"gx": gx, "gy": xs[1] * 2 + h}
    left = {"gx": gx, "gy": xs[3] * 2 + h}
    far = {"gx": gx, "gy": x * 2 + (1 - h)}
    g_next = {"gx": (gx + 1) % n_gx, "gy": gy}
    g_prev = {"gx": (gx + n_gx - 1) % n_gx, "gy": gy}

    started = []

    def message(i, src, dst, dev):
        return pltpu.make_async_remote_copy(
            src_ref=src, dst_ref=dst, send_sem=send_sem.at[i], recv_sem=recv_sem.at[i],
            device_id=dev, device_id_type=MESH,
        )

    def send(i, src, dst, dev):
        copy = message(i, src, dst, dev)
        copy.start()
        started.append(copy)

    def arrived(i, dst, dev):
        message(i, dst, dst, dev).wait_recv()

    load_a = pltpu.make_async_copy(a_hbm, aj.at[pl.ds(0, rows)], local_sem.at[0])
    load_j = pltpu.make_async_copy(j_hbm, aj.at[pl.ds(rows, rows)], local_sem.at[1])
    load_scale = pltpu.make_async_copy(scale_hbm, scale_ref, local_sem.at[2])
    load_shock = pltpu.make_async_copy(shock_hbm, shock_ref, local_sem.at[3])
    load_scale.start()
    load_a.start()
    load_j.start()
    load_shock.start()

    barrier = pltpu.get_barrier_semaphore()
    for dev in (right, left, far, g_next, g_prev):
        pl.semaphore_signal(barrier, inc=1, device_id=dev, device_id_type=MESH)
    pl.semaphore_wait(barrier, 5)

    AG_Z, RS_Z = 4, 8
    AG_OWN, AG_FAR, RS_FAR, RS_OWN = 12, 24, 36, 48
    z_order = [p for i in range(n_up) for p in (i, n_up + i)]

    def spread(base, source, g, pieces):
        for p in pieces:
            send(base + p, source.at[span[p]], qb.at[g, span[p]], right)
        for p in pieces:
            q = (p + n_up) % N_PIECE
            send(base + 4 + q, source.at[span[q]], qb.at[g, span[q]], left)

    def pass_on(base, hh, i):
        gl, gr, j = xs[3] * 2 + hh, xs[1] * 2 + hh, n_up + i
        arrived(base + i, qb.at[gl, span[i]], left)
        send(base + 8 + i, qb.at[gl, span[i]], qb.at[gl, span[i]], right)
        arrived(base + 4 + j, qb.at[gr, span[j]], right)
        send(base + 8 + j, qb.at[gr, span[j]], qb.at[gr, span[j]], left)

    for p in z_order:
        send(AG_Z + p, q_ref.at[span[p]], qb.at[gy, span[p]], far)
    spread(AG_OWN, q_ref, gy, range(n_up))
    send(0, w_ref, wl, g_next)
    send(1, w_ref, wr, g_prev)
    spread(AG_OWN, q_ref, gy, range(n_up, N_PIECE))
    qb[gy] = q_ref[...]

    has_prev = jnp.where(gx > 0, 1.0, 0.0).astype(f32)
    has_next = jnp.where(gx < n_gx - 1, 1.0, 0.0).astype(f32)
    for i in range(n_up):
        pass_on(AG_OWN, h, i)
    arrived(0, wl, g_prev)
    arrived(1, wr, g_next)
    w0, w1 = w_ref[:, c0].astype(f32), w_ref[:, c1].astype(f32)
    l0, l1 = wl[:, c0].astype(f32) * has_prev, wl[:, c1].astype(f32) * has_prev
    r0, r1 = wr[:, c0].astype(f32) * has_next, wr[:, c1].astype(f32) * has_next
    load_scale.wait()
    scale = scale_ref[...].T
    s0, s1 = scale[:, 0:1], scale[:, 1:2]
    sb[pl.ds(0, rows), c0] = (s0 * w0).astype(bf16)
    sb[pl.ds(0, rows), c1] = (s1 * w1).astype(bf16)
    sb[pl.ds(rows, rows), c0] = (((FAR * r0 - NEAR * w1) + NEAR * l1) - FAR * l0).astype(bf16)
    sb[pl.ds(rows, rows), c1] = (((FAR * r1 - NEAR * r0) + NEAR * w0) - FAR * l1).astype(bf16)
    load_a.wait()
    load_j.wait()

    def columns(d):
        return pl.ds(pl.multiple_of(xs[d] * (2 * rows), 128), 2 * rows)

    def transposed_block(d):
        t = lax.dot_general(
            aj[:, columns(d)], sb[...], (((0,), (0,)), ((), ())), preferred_element_type=f32
        ).astype(bf16)
        tb[2 * d] = t[:rows]
        tb[2 * d + 1] = t[rows:]

    def first_far(k, base):
        part = 4 + (1 - h if k == 0 else h)
        for i in range(n_up):
            j = n_up + i
            send(base + i, tb.at[part, span[i]], rx.at[k, 0, 0, i], right)
            send(base + j, tb.at[part, span[j]], rx.at[k, 1, 0, i], left)

    def first_near(k, base):
        hh = 1 - h if k == 0 else h
        for i in range(n_up):
            j = n_up + i
            send(base + 4 + j, tb.at[2 + hh, span[j]], rx.at[k, 0, 1, i], right)
            send(base + 4 + i, tb.at[6 + hh, span[i]], rx.at[k, 1, 1, i], left)

    def second(k, base, i):
        hh = 1 - h if k == 0 else h
        j = n_up + i
        arrived(base + i, rx.at[k, 0, 0, i], left)
        acc[k, i] = (tb[2 + hh, span[i], :].astype(f32) + rx[k, 0, 0, i].astype(f32)).astype(bf16)
        arrived(base + j, rx.at[k, 1, 0, i], right)
        acc[k, j] = (tb[6 + hh, span[j], :].astype(f32) + rx[k, 1, 0, i].astype(f32)).astype(bf16)
        send(base + 8 + i, acc.at[k, i], rx.at[k, 0, 2, i], right)
        send(base + 8 + j, acc.at[k, j], rx.at[k, 1, 2, i], left)

    def summed(k, base, p):
        hh = 1 - h if k == 0 else h
        i = p % n_up
        side = 1 if p < n_up else 0
        arrived(base + 4 + p, rx.at[k, side, 1, i], right if side else left)
        arrived(base + 8 + p, rx.at[k, 1 - side, 2, i], left if side else right)
        return (tb[hh, span[p], :].astype(f32) + rx[k, 1 - side, 2, i].astype(f32)) + rx[
            k, side, 1, i
        ].astype(f32)

    transposed_block(2)
    transposed_block(1)
    first_far(0, RS_FAR)
    transposed_block(3)
    first_near(0, RS_FAR)
    transposed_block(0)

    gp = x * 2 + (1 - h)

    def from_partner(i):
        for p in (i, n_up + i):
            arrived(AG_Z + p, qb.at[gp, span[p]], far)
        spread(AG_FAR, qb.at[gp], gp, [i])
        spread(AG_FAR, qb.at[gp], gp, [n_up + i])

    from_partner(0)
    second(0, RS_FAR, 0)
    second(0, RS_FAR, 1)
    from_partner(1)
    for p in z_order:
        zs[span[p], :] = summed(0, RS_FAR, p).astype(bf16)
        send(RS_Z + p, zs.at[span[p]], rz.at[span[p]], far)

    def forward_block(d):
        part = jnp.dot(
            aj[:, columns(d)],
            qb[pl.ds(xs[d] * 2, 2)].reshape(2 * rows, flat),
            preferred_element_type=f32,
        )
        facc[...] = part if d == 0 else facc[...] + part

    for i in range(n_up):
        pass_on(AG_FAR, 1 - h, i)
    first_far(1, RS_OWN)
    first_near(1, RS_OWN)
    forward_block(0)

    def whole_from(d, dev, base):
        for hh, first in ((h, AG_OWN), (1 - h, AG_FAR)):
            for p in range(N_PIECE):
                done = (p < n_up) == (base == 0)
                if not done:
                    arrived(first + base + p, qb.at[xs[d] * 2 + hh, span[p]], dev)
        forward_block(d)

    whole_from(3, left, 0)
    whole_from(1, right, 4)
    for hh, first in ((h, AG_OWN), (1 - h, AG_FAR)):
        for p in range(N_PIECE):
            arrived(first + 8 + p, qb.at[xs[2] * 2 + hh, span[p]], left if p < n_up else right)
    forward_block(2)

    def sigma(offset):
        station = gx * 2 + offset
        hit = jnp.where(shock_ref[0] == station, 1.0, 0.0)
        for k in range(1, shock_ref.shape[0]):
            hit = jnp.where(shock_ref[k] == station, 1.0, hit)
        return hit.astype(f32)

    load_shock.wait()
    sig = [sigma(o) for o in (-1, 0, 1, 2)]
    q0, q1 = q_ref[:, c0].astype(f32), q_ref[:, c1].astype(f32)
    flux = pl.ds(rows, rows)
    p0, p1 = facc[flux, c0], facc[flux, c1]
    pn[0, :, c0] = ((FAR * p0 - NEAR * p1) + (SHOCK_GAIN * sig[3]) * q1).astype(bf16)
    pn[0, :, c1] = (FAR * p1).astype(bf16)
    pn[1, :, c0] = (-FAR * p0).astype(bf16)
    pn[1, :, c1] = ((NEAR * p0 - FAR * p1) + (SHOCK_GAIN * sig[0]) * q0).astype(bf16)
    send(2, pn.at[0], pr.at[0], g_next)
    send(3, pn.at[1], pr.at[1], g_prev)

    second(1, RS_OWN, 0)
    second(1, RS_OWN, 1)
    add0 = SHOCK_GAIN * ((sig[0] * l1 - 2.0 * sig[1] * w0) + sig[2] * w1)
    add1 = SHOCK_GAIN * ((sig[1] * w0 - 2.0 * sig[2] * w1) + sig[3] * r0)
    for p in z_order:
        term = summed(1, RS_OWN, p)
        arrived(RS_Z + p, rz.at[span[p]], far)
        term = term + rz[span[p], :].astype(f32)
        own = slice(p * tall, (p + 1) * tall)
        ao_ref[span[p], c0] = (term[:, c0] + add0[own]).astype(bf16)
        ao_ref[span[p], c1] = (term[:, c1] + add1[own]).astype(bf16)

    base0 = s0 * facc[pl.ds(0, rows), c0] + NEAR * p1 + (SHOCK_GAIN * sig[1]) * (q1 - 2.0 * q0)
    base1 = s1 * facc[pl.ds(0, rows), c1] - NEAR * p0 + (SHOCK_GAIN * sig[2]) * (q0 - 2.0 * q1)
    arrived(2, pr.at[0], g_prev)
    arrived(3, pr.at[1], g_next)
    fo_ref[:, c0] = (
        base0 + has_prev * pr[0, :, c0].astype(f32) + has_next * pr[1, :, c0].astype(f32)
    ).astype(bf16)
    fo_ref[:, c1] = (
        base1 + has_prev * pr[0, :, c1].astype(f32) + has_next * pr[1, :, c1].astype(f32)
    ).astype(bf16)

    for copy in started:
        copy.wait_send()


def local(n_gx, q, w, row_scale, station_block, jacobian_block, shock_stations):
    rows, count, width = q.shape
    flat = count * width
    total = station_block.shape[1]
    bf16 = jnp.bfloat16
    vmem = pl.BlockSpec(memory_space=pltpu.VMEM)
    hbm = pl.BlockSpec(memory_space=pltpu.HBM)
    tall = rows // N_PIECE
    out = jax.ShapeDtypeStruct((rows, flat), bf16)
    fo, ao = pl.pallas_call(
        functools.partial(kernel, n_gx),
        out_shape=(out, out),
        in_specs=[vmem, vmem, hbm, hbm, hbm, hbm],
        out_specs=(vmem, vmem),
        scratch_shapes=[
            pltpu.VMEM((count, rows), jnp.float32),
            pltpu.SMEM(shock_stations.shape, jnp.int32),
            pltpu.VMEM((2 * rows, total), bf16),
            pltpu.VMEM((2 * N_X, rows, flat), bf16),
            pltpu.VMEM((2 * N_X, rows, flat), bf16),
            pltpu.VMEM((2 * rows, flat), bf16),
            pltpu.VMEM((2 * rows, flat), jnp.float32),
            pltpu.VMEM((rows, flat), bf16),
            pltpu.VMEM((rows, flat), bf16),
            pltpu.VMEM((2, 2, 3, N_PIECE // 2, tall, flat), bf16),
            pltpu.VMEM((2, N_PIECE, tall, flat), bf16),
            pltpu.VMEM((rows, flat), bf16),
            pltpu.VMEM((rows, flat), bf16),
            pltpu.VMEM((2, rows, flat), bf16),
            pltpu.VMEM((2, rows, flat), bf16),
            pltpu.SemaphoreType.DMA((4,)),
            pltpu.SemaphoreType.DMA((N_MSG,)),
            pltpu.SemaphoreType.DMA((N_MSG,)),
        ],
        compiler_params=pltpu.CompilerParams(
            collective_id=0, has_side_effects=True, vmem_limit_bytes=63 * 1024 * 1024
        ),
    )(
        q.reshape(rows, flat), w.reshape(rows, flat), row_scale.T, shock_stations,
        station_block, jacobian_block,
    )
    return fo.reshape(rows, count, width), ao.reshape(rows, count, width)


def solution(mesh):
    in_specs = (
        P("gy", "gx", None),
        P("gy", "gx", None),
        P("gy", "gx"),
        P("gy", None),
        P("gy", None),
        P(),
    )
    out_specs = (P("gy", "gx", None), P("gy", "gx", None))
    return jax.shard_map(
        functools.partial(local, mesh.shape["gx"]),
        mesh=mesh, in_specs=in_specs, out_specs=out_specs, check_vma=False,
    )
```

time: 51 us -> 48.2 us (0.945)
  local copies, waits for them, and re-layouts: 6.78 us -> 5.01 us
  Pallas kernels: 43.3 us -> 42.1 us
    unnamed x7 -> x0, local copies, waits for them, and re-layouts: 4.33 us -> none
    reshape x2, local copies, waits for them, and re-layouts: 1.42 us -> 3.25 us  [local(): return (fo.reshape(rows, count, width), ao.reshape(rows, count, width))]
    pallas_call x1, Pallas kernels: 43.3 us -> 42.1 us  [local(): pl.pallas_call(functools.partial(kernel, n_gx), out_shape=(out, out), in_...]
    reshape x1, local copies, waits for them, and re-layouts: 1.04 us -> 1.76 us  [local(): w.reshape(rows, flat)]
where the time goes in v2:
time: 48.2 us; the launch traced here: 47.8 us
  Pallas kernels  42.1 us (87%)
  local copies, waits for them, and re-layouts  5.01 us (10%)
  between operations  0.64 us (1%)
    pallas_call x1, Pallas kernels, local(): pl.pallas_call(functools.partial(kernel, n_gx), out_shape=(out, out), in_...  42.1 us
    reshape x2, local copies, waits for them, and re-layouts, local(): return (fo.reshape(rows, count, width), ao.reshape(rows, count, width))  3.25 us
    reshape x1, local copies, waits for them, and re-layouts, local(): w.reshape(rows, flat)  1.76 us

profile of v2, /device:TPU:6, one launch (start us, length us, event | category | flops | bytes accessed | tf_op | source)
XLA Modules:
  0.0 47.8 jit_solution(11204976721323731026)
XLA Ops:
  0.6 1.8 %copy_bitcast_fusion = (bf16[320,256]{1,0:T(8,128)(2,1)}, bf16[320,256]{1,0:T(8,128)(2,1)}) fusion(bf16[40,8,2,128]{3,2,1,0:T(2,128)(2,1)} %bitcast.7, bf16[40,8,2,128]{3,2,1,0:T(2,128)(2,1)} %bitcast.8), kind=kLoop, calls=%fused_computation | loop fusion | bytes 655360 | tf_op jit(solution)/shard_map/reshape | solution.py:301
  2.4 42.1 %shard_map.77 = (bf16[320,256]{1,0:T(8,128)(2,1)}, bf16[320,256]{1,0:T(8,128)(2,1)}) custom-call(bf16[320,256]{1,0:T(8,128)(2,1)} %get-tuple-element.7.q_ref, bf16[320,256]{1,0:T(8,128)(2,1)} %get-tuple-element.6.w_ref, f32[2,320]{1,0:T(2,128)} %bitcast.9, s32[16]{0:T(128)} %shock_hbm.1, bf16[320,2560]{1,0:T(8,128)(2,1)} %a_hbm.1, bf16[320,2560]{1,0:T(8,128)(2,1)} %j_hbm.1), custom_call_target="tpu_custom_call" | custom-call | tf_op jit(solution)/shard_map/pallas_call | solution.py:272
  44.5 1.6 %reshape.18 = bf16[320,2,128]{2,1,0:T(2,128)(2,1)} reshape(bf16[320,256]{1,0:T(8,128)(2,1)} %get-tuple-element.4) | data formatting | bytes 327680 | tf_op jit(solution)/shard_map/reshape | solution.py:304
  46.1 1.6 %reshape.19 = bf16[320,2,128]{2,1,0:T(2,128)(2,1)} reshape(bf16[320,256]{1,0:T(8,128)(2,1)} %get-tuple-element.5) | data formatting | bytes 327680 | tf_op jit(solution)/shard_map/reshape | solution.py:304

commit v3 on v2

--- a/solution.py
+++ b/solution.py
@@ -295,11 +295,12 @@
             pltpu.SemaphoreType.DMA((N_MSG,)),
         ],
         compiler_params=pltpu.CompilerParams(
-            collective_id=0, has_side_effects=True, vmem_limit_bytes=63 * 1024 * 1024
+            collective_id=0, has_side_effects=True, vmem_limit_bytes=40 * 1024 * 1024
         ),
     )(
-        q.reshape(rows, flat), w.reshape(rows, flat), row_scale.T, shock_stations,
-        station_block, jacobian_block,
+        q.reshape(rows, flat), w.reshape(rows, flat),
+        *(pltpu.with_memory_space_constraint(v, pltpu.HBM)
+          for v in (row_scale.T, shock_stations, station_block, jacobian_block)),
     )
     return fo.reshape(rows, count, width), ao.reshape(rows, count, width)
 

time: 48.2 us -> 44 us (0.913)
  local copies, waits for them, and re-layouts: 5.01 us -> 2.45 us
  Pallas kernels: 42.1 us -> 40.5 us
    reshape x2, local copies, waits for them, and re-layouts: 3.25 us -> 1.42 us  [local(): return (fo.reshape(rows, count, width), ao.reshape(rows, count, width))]
    pallas_call x1, Pallas kernels: 42.1 us -> 40.5 us  [local(): pl.pallas_call(functools.partial(kernel, n_gx), out_shape=(out, out), in_...]
    reshape x1, local copies, waits for them, and re-layouts: 1.76 us -> 1.04 us  [local(): w.reshape(rows, flat)]
where the time goes in v3:
time: 44 us; the launch traced here: 43.6 us
  Pallas kernels  40.5 us (92%)
  local copies, waits for them, and re-layouts  2.45 us (6%)
  between operations  0.64 us (1%)
    pallas_call x1, Pallas kernels, local(): pl.pallas_call(functools.partial(kernel, n_gx), out_shape=(out, out), in_...  40.5 us
    reshape x2, local copies, waits for them, and re-layouts, local(): return (fo.reshape(rows, count, width), ao.reshape(rows, count, width))  1.42 us
    reshape x1, local copies, waits for them, and re-layouts, local(): w.reshape(rows, flat)  1.04 us

profile of v3, /device:TPU:6, one launch (start us, length us, event | category | flops | bytes accessed | tf_op | source)
XLA Modules:
  0.0 43.6 jit_solution(12487399366078360479)
XLA Ops:
  0.6 1.0 %copy_bitcast_fusion = (bf16[320,256]{1,0:T(8,128)(2,1)S(1)}, bf16[320,256]{1,0:T(8,128)(2,1)S(1)}) fusion(bf16[40,8,2,128]{3,2,1,0:T(2,128)(2,1)} %bitcast.7, bf16[40,8,2,128]{3,2,1,0:T(2,128)(2,1)} %bitcast.8), kind=kLoop, calls=%fused_computation | loop fusion | bytes 655360 | tf_op jit(solution)/shard_map/reshape | solution.py:301
  1.7 40.5 %shard_map.77 = (bf16[320,256]{1,0:T(8,128)(2,1)S(1)}, bf16[320,256]{1,0:T(8,128)(2,1)S(1)}) custom-call(bf16[320,256]{1,0:T(8,128)(2,1)S(1)} %get-tuple-element.7.q_ref, bf16[320,256]{1,0:T(8,128)(2,1)S(1)} %get-tuple-element.6.w_ref, f32[2,320]{1,0:T(2,128)} %bitcast.9, s32[16]{0:T(128)} %shock_hbm.1, bf16[320,2560]{1,0:T(8,128)(2,1)} %a_hbm.1, ...), custom_call_target="tpu_custom_call" | custom-call | tf_op jit(solution)/shard_map/pallas_call | solution.py:272
  42.2 0.7 %reshape.18 = bf16[320,2,128]{2,1,0:T(2,128)(2,1)} reshape(bf16[320,256]{1,0:T(8,128)(2,1)S(1)} %get-tuple-element.4) | data formatting | bytes 327680 | tf_op jit(solution)/shard_map/reshape | solution.py:305
  42.9 0.7 %reshape.19 = bf16[320,2,128]{2,1,0:T(2,128)(2,1)} reshape(bf16[320,256]{1,0:T(8,128)(2,1)S(1)} %get-tuple-element.5) | data formatting | bytes 327680 | tf_op jit(solution)/shard_map/reshape | solution.py:305

commit v4 on v3

--- a/solution.py
+++ b/solution.py
@@ -44,6 +44,8 @@
     g_prev = {"gx": (gx + n_gx - 1) % n_gx, "gy": gy}
 
     started = []
+    first, last = gx == 0, gx == n_gx - 1
+    inner_prev, inner_next = jnp.logical_not(first), jnp.logical_not(last)
 
     def message(i, src, dst, dev):
         return pltpu.make_async_remote_copy(
@@ -55,6 +57,16 @@
         copy = message(i, src, dst, dev)
         copy.start()
         started.append(copy)
+
+    def send_along(there, i, src, dst, dev):
+        @pl.when(there)
+        def _():
+            message(i, src, dst, dev).start()
+
+    def arrived_along(there, i, dst, dev):
+        @pl.when(there)
+        def _():
+            message(i, dst, dst, dev).wait_recv()
 
     def arrived(i, dst, dev):
         message(i, dst, dst, dev).wait_recv()
@@ -69,9 +81,21 @@
     load_shock.start()
 
     barrier = pltpu.get_barrier_semaphore()
-    for dev in (right, left, far, g_next, g_prev):
+    for dev in (right, left, far):
         pl.semaphore_signal(barrier, inc=1, device_id=dev, device_id_type=MESH)
-    pl.semaphore_wait(barrier, 5)
+    for there, dev in ((inner_prev, g_prev), (inner_next, g_next)):
+        @pl.when(there)
+        def _(dev=dev):
+            pl.semaphore_signal(barrier, inc=1, device_id=dev, device_id_type=MESH)
+    inside = jnp.logical_and(inner_prev, inner_next)
+
+    @pl.when(inside)
+    def _():
+        pl.semaphore_wait(barrier, 5)
+
+    @pl.when(jnp.logical_not(inside))
+    def _():
+        pl.semaphore_wait(barrier, 4)
 
     AG_Z, RS_Z = 4, 8
     AG_OWN, AG_FAR, RS_FAR, RS_OWN = 12, 24, 36, 48
@@ -94,20 +118,29 @@
     for p in z_order:
         send(AG_Z + p, q_ref.at[span[p]], qb.at[gy, span[p]], far)
     spread(AG_OWN, q_ref, gy, range(n_up))
-    send(0, w_ref, wl, g_next)
-    send(1, w_ref, wr, g_prev)
+    send_along(inner_next, 0, w_ref, wl, g_next)
+    send_along(inner_prev, 1, w_ref, wr, g_prev)
     spread(AG_OWN, q_ref, gy, range(n_up, N_PIECE))
     qb[gy] = q_ref[...]
 
-    has_prev = jnp.where(gx > 0, 1.0, 0.0).astype(f32)
-    has_next = jnp.where(gx < n_gx - 1, 1.0, 0.0).astype(f32)
+    @pl.when(first)
+    def _():
+        wl[...] = jnp.zeros_like(wl)
+        pr[0] = jnp.zeros(pr.shape[1:], bf16)
+
+    @pl.when(last)
+    def _():
+        wr[...] = jnp.zeros_like(wr)
+        pr[1] = jnp.zeros(pr.shape[1:], bf16)
+
+
     for i in range(n_up):
         pass_on(AG_OWN, h, i)
-    arrived(0, wl, g_prev)
-    arrived(1, wr, g_next)
+    arrived_along(inner_prev, 0, wl, g_prev)
+    arrived_along(inner_next, 1, wr, g_next)
     w0, w1 = w_ref[:, c0].astype(f32), w_ref[:, c1].astype(f32)
-    l0, l1 = wl[:, c0].astype(f32) * has_prev, wl[:, c1].astype(f32) * has_prev
-    r0, r1 = wr[:, c0].astype(f32) * has_next, wr[:, c1].astype(f32) * has_next
+    l0, l1 = wl[:, c0].astype(f32), wl[:, c1].astype(f32)
+    r0, r1 = wr[:, c0].astype(f32), wr[:, c1].astype(f32)
     load_scale.wait()
     scale = scale_ref[...].T
     s0, s1 = scale[:, 0:1], scale[:, 1:2]
@@ -177,14 +210,6 @@
         spread(AG_FAR, qb.at[gp], gp, [i])
         spread(AG_FAR, qb.at[gp], gp, [n_up + i])
 
-    from_partner(0)
-    second(0, RS_FAR, 0)
-    second(0, RS_FAR, 1)
-    from_partner(1)
-    for p in z_order:
-        zs[span[p], :] = summed(0, RS_FAR, p).astype(bf16)
-        send(RS_Z + p, zs.at[span[p]], rz.at[span[p]], far)
-
     def forward_block(d):
         part = jnp.dot(
             aj[:, columns(d)],
@@ -193,8 +218,19 @@
         )
         facc[...] = part if d == 0 else facc[...] + part
 
-    for i in range(n_up):
-        pass_on(AG_FAR, 1 - h, i)
+    def reduced(i):
+        for p in (i, n_up + i):
+            zs[span[p], :] = summed(0, RS_FAR, p).astype(bf16)
+            send(RS_Z + p, zs.at[span[p]], rz.at[span[p]], far)
+
+    second(0, RS_FAR, 0)
+    from_partner(0)
+    second(0, RS_FAR, 1)
+    from_partner(1)
+    reduced(0)
+    pass_on(AG_FAR, 1 - h, 0)
+    reduced(1)
+    pass_on(AG_FAR, 1 - h, 1)
     first_far(1, RS_OWN)
     first_near(1, RS_OWN)
     forward_block(0)
@@ -230,8 +266,8 @@
     pn[0, :, c1] = (FAR * p1).astype(bf16)
     pn[1, :, c0] = (-FAR * p0).astype(bf16)
     pn[1, :, c1] = ((NEAR * p0 - FAR * p1) + (SHOCK_GAIN * sig[0]) * q0).astype(bf16)
-    send(2, pn.at[0], pr.at[0], g_next)
-    send(3, pn.at[1], pr.at[1], g_prev)
+    send_along(inner_next, 2, pn.at[0], pr.at[0], g_next)
+    send_along(inner_prev, 3, pn.at[1], pr.at[1], g_prev)
 
     second(1, RS_OWN, 0)
     second(1, RS_OWN, 1)
@@ -247,17 +283,24 @@
 
     base0 = s0 * facc[pl.ds(0, rows), c0] + NEAR * p1 + (SHOCK_GAIN * sig[1]) * (q1 - 2.0 * q0)
     base1 = s1 * facc[pl.ds(0, rows), c1] - NEAR * p0 + (SHOCK_GAIN * sig[2]) * (q0 - 2.0 * q1)
-    arrived(2, pr.at[0], g_prev)
-    arrived(3, pr.at[1], g_next)
+    arrived_along(inner_prev, 2, pr.at[0], g_prev)
+    arrived_along(inner_next, 3, pr.at[1], g_next)
     fo_ref[:, c0] = (
-        base0 + has_prev * pr[0, :, c0].astype(f32) + has_next * pr[1, :, c0].astype(f32)
+        base0 + pr[0, :, c0].astype(f32) + pr[1, :, c0].astype(f32)
     ).astype(bf16)
     fo_ref[:, c1] = (
-        base1 + has_prev * pr[0, :, c1].astype(f32) + has_next * pr[1, :, c1].astype(f32)
+        base1 + pr[0, :, c1].astype(f32) + pr[1, :, c1].astype(f32)
     ).astype(bf16)
 
     for copy in started:
         copy.wait_send()
+    for there, i, src, dev in (
+        (inner_next, 0, w_ref, g_next), (inner_prev, 1, w_ref, g_prev),
+        (inner_next, 2, pn.at[0], g_next), (inner_prev, 3, pn.at[1], g_prev),
+    ):
+        @pl.when(there)
+        def _(i=i, src=src, dev=dev):
+            message(i, src, src, dev).wait_send()
 
 
 def local(n_gx, q, w, row_scale, station_block, jacobian_block, shock_stations):

time: 44 us -> 42.7 us (0.970)
  the two profiles are of different devices: /device:TPU:6 before, /device:TPU:25 now
where the time goes in v4:
time: 42.7 us; the launch traced here: 42.6 us
  Pallas kernels  39.5 us (93%)
  local copies, waits for them, and re-layouts  2.45 us (6%)
  between operations  0.64 us (1%)
    pallas_call x1, Pallas kernels, local(): pl.pallas_call(functools.partial(kernel, n_gx), out_shape=(out, out), in_...  39.5 us
    reshape x2, local copies, waits for them, and re-layouts, local(): return (fo.reshape(rows, count, width), ao.reshape(rows, count, width))  1.42 us
    reshape x1, local copies, waits for them, and re-layouts, local(): w.reshape(rows, flat)  1.04 us

profile of v4, /device:TPU:25, one launch (start us, length us, event | category | flops | bytes accessed | tf_op | source)
XLA Modules:
  0.0 42.6 jit_solution(4147004613764633217)
XLA Ops:
  0.6 1.0 %copy_bitcast_fusion = (bf16[320,256]{1,0:T(8,128)(2,1)S(1)}, bf16[320,256]{1,0:T(8,128)(2,1)S(1)}) fusion(bf16[40,8,2,128]{3,2,1,0:T(2,128)(2,1)} %bitcast.7, bf16[40,8,2,128]{3,2,1,0:T(2,128)(2,1)} %bitcast.8), kind=kLoop, calls=%fused_computation | loop fusion | bytes 655360 | tf_op jit(solution)/shard_map/reshape | solution.py:344
  1.7 39.5 %shard_map.77 = (bf16[320,256]{1,0:T(8,128)(2,1)S(1)}, bf16[320,256]{1,0:T(8,128)(2,1)S(1)}) custom-call(bf16[320,256]{1,0:T(8,128)(2,1)S(1)} %get-tuple-element.7.q_ref, bf16[320,256]{1,0:T(8,128)(2,1)S(1)} %get-tuple-element.6.w_ref, f32[2,320]{1,0:T(2,128)} %bitcast.9, s32[16]{0:T(128)} %shock_hbm.1, bf16[320,2560]{1,0:T(8,128)(2,1)} %a_hbm.1, ...), custom_call_target="tpu_custom_call" | custom-call | tf_op jit(solution)/shard_map/pallas_call | solution.py:315
  41.2 0.7 %reshape.18 = bf16[320,2,128]{2,1,0:T(2,128)(2,1)} reshape(bf16[320,256]{1,0:T(8,128)(2,1)S(1)} %get-tuple-element.4) | data formatting | bytes 327680 | tf_op jit(solution)/shard_map/reshape | solution.py:348
  41.9 0.7 %reshape.19 = bf16[320,2,128]{2,1,0:T(2,128)(2,1)} reshape(bf16[320,256]{1,0:T(8,128)(2,1)S(1)} %get-tuple-element.5) | data formatting | bytes 327680 | tf_op jit(solution)/shard_map/reshape | solution.py:348
